TPU v7x, 32 devices: a whole 2x2x4 slice. The times are simulated.
32 devices in a mesh: blk: 8 (over y, x, core), rows: 4 (over z).
Axes of the slice: x: 2, y: 2, z: 4, core: 2. Of those that a mesh axis runs over, the one named last changes fastest.
Arguments:
- cholesky: bfloat16 [4096, 256, 256], P('blk', 'rows'), may hold values from -0.01171875 to 0.01171875
- green: bfloat16 [256, 256, 256], P('blk', 'rows'), may hold values from -18 to 18
- aux_field: float32 [256, 4096], P(None, 'blk'), may hold values from -6 to 6
- walker_orbitals: bfloat16 [256, 256, 128], P('blk', 'rows'), may hold values from -6 to 6
Outputs:
- new_orbitals: float32 [256, 256, 128], P('blk', 'rows')
- force_bias: float32 [256, 4096], P(None, 'blk')
All inputs are finite; a program needn't handle non-finite values.
Results may differ from a plain program's by a relative error of at most 0.025.
Values may be sent and summed in bfloat16 or wider, within the bound.
No kernel may reach another device: no remote copies, remote signals or barrier semaphores. Data moves between devices by JAX's collectives and lax.ppermute only.
A program may use at most 128 MiB of HBM per device.

v0:
```python
import jax
import jax.numpy as jnp
from jax import lax
from jax.sharding import PartitionSpec as P

TAYLOR = 4
time_root = 0.5


def shards(cholesky, green, aux_field, walker_orbitals):
    ch_dev, rows_dev, orbitals = cholesky.shape
    flat_chol = cholesky.reshape(ch_dev, rows_dev * orbitals)
    walk_count = walker_orbitals.shape[0]
    batch_piece = lax.all_gather(green, "blk", axis=0, tiled=True)
    flat_piece = batch_piece.reshape(batch_piece.shape[0], rows_dev * orbitals)
    partial_bias = lax.dot_general(
        flat_piece, flat_chol, (((1,), (1,)), ((), ())), preferred_element_type=jnp.float32
    )
    force_bias = lax.psum(partial_bias.astype(jnp.bfloat16), "rows").astype(jnp.float32)
    shifted = (time_root * (aux_field - force_bias)).astype(jnp.bfloat16)
    summed = lax.psum_scatter(
        jnp.dot(shifted, flat_chol, preferred_element_type=jnp.float32).astype(jnp.bfloat16),
        "blk",
        scatter_dimension=0,
        tiled=True,
    )
    potential = summed.reshape(walk_count, rows_dev, orbitals)
    result = walker_orbitals.astype(jnp.float32)
    full_potential = lax.all_gather(potential, "rows", axis=1, tiled=True)
    full_term = lax.all_gather(walker_orbitals, "rows", axis=1, tiled=True)
    offset = lax.axis_index("rows") * rows_dev
    for degree in range(1, TAYLOR + 1):
        product = jnp.einsum(
            "wik,wka->wia", full_potential, full_term, preferred_element_type=jnp.float32
        )
        full_term = (product / degree).astype(jnp.bfloat16)
        own_rows = lax.dynamic_slice_in_dim(full_term, offset, rows_dev, 1)
        result = result + own_rows.astype(jnp.float32)
    return (result, force_bias)


def solution(mesh):
    return jax.shard_map(
        shards,
        mesh=mesh,
        in_specs=(
            P("blk", "rows", None),
            P("blk", "rows", None),
            P(None, "blk"),
            P("blk", "rows", None),
        ),
        out_specs=(P("blk", "rows", None), P(None, "blk")),
        check_vma=False,
    )
```

profile of v0, /device:TPU:0, one launch (start us, length us, event | category | flops | bytes accessed | tf_op | source)
XLA Modules:
  0.0 360.4 jit_solution(13983244792735845269)
XLA Ops:
  7.2 0.0 all-gather.4.cloned.1.call-start
  7.2 2.8 copy.6
  10.0 0.0 all-gather.4.cloned.1.call-update
  10.0 0.0 all-reduce.2.cloned.1.call-start
  10.1 57.4 %all-gather.4.cloned.1.call-done = bf16[256,64,256]{2,0,1:T(8,128)(2,1)} async-done(((bf16[32,64,256]{2,0,1:T(8,128)(2,1)}), bf16[256,64,256]{2,0,1:T(8,128)(2,1)}) %all-gather.4.cloned.1.call-update) | async-done | bytes 8388624 | tf_op jit(solution)/shard_map/all_gather | solution.py:14
  67.5 27.3 %fusion.5 = bf16[256,512]{1,0:T(8,128)(2,1)} fusion(bf16[256,64,256]{2,0,1:T(8,128)(2,1)} %all-gather.4.cloned.1.call-done, bf16[512,64,256]{2,1,0:T(8,128)(2,1)} %param.4), kind=kOutput, calls=%fused_computation.7 | convolution fusion | flops 4295098368 | bytes 25427968 | tf_op jit(solution)/shard_map/dot_general | solution.py:16
  94.7 0.0 all-reduce.2.cloned.1.call-update
  94.7 0.0 reduce-scatter.2.cloned.1.call-start
  94.8 0.0 copy-start.3
  94.8 17.9 %copy.8 = bf16[64,8,64,256]{3,1,2,0:T(8,128)(2,1)} copy(bf16[64,8,64,256]{3,2,1,0:T(8,128)(2,1)} %bitcast.19) | data formatting | bytes 33554432
  112.7 17.8 %all-reduce.2.cloned.1.call-done = bf16[256,512]{1,0:T(8,128)(2,1)} async-done(((bf16[256,512]{1,0:T(8,128)(2,1)}), bf16[256,512]{1,0:T(8,128)(2,1)}) %all-reduce.2.cloned.1.call-update) | async-done | bytes 262160 | tf_op jit(solution)/shard_map/psum | solution.py:19
  130.5 1.0 convert_element_type.41
  131.5 0.0 copy-start.2
  131.5 0.0 copy-done.3
  131.5 12.7 %convolution_convert_fusion = bf16[256,16384]{1,0:T(8,128)(2,1)} fusion(bf16[512,16384]{1,0:T(8,128)(2,1)} %bitcast.18, f32[256,512]{1,0:T(8,128)S(1)} %copy-done.3, f32[256,512]{1,0:T(8,128)S(1)} %convert_element_type.41), kind=kOutput, calls=%fused_computation | convolution fusion | flops 4299554816 | bytes 26214400 | tf_op jit(solution)/shard_map/dot_general | solution.py:22
  144.2 0.0 copy-done.2
  144.2 0.0 reduce-scatter.2.cloned.1.call-update
  144.2 0.0 all-gather.8.cloned.1.call-start
  144.3 0.5 all-gather.8.cloned.1.call-update
  144.8 0.3 all-gather.6.cloned.1.call-start
  145.1 70.7 %reduce-scatter.2.cloned.1.call-done = bf16[32,16384]{1,0:T(8,128)(2,1)} async-done(((bf16[256,16384]{1,0:T(8,128)(2,1)}), bf16[32,16384]{1,0:T(8,128)(2,1)}) %reduce-scatter.2.cloned.1.call-update) | async-done | bytes 1048592 | tf_op jit(solution)/shard_map/reduce_scatter | solution.py:21
  215.7 2.4 copy.9
  218.2 0.0 all-gather.6.cloned.1.call-update
  218.2 44.7 %all-gather.8.cloned.1.call-done = bf16[32,256,128]{2,1,0:T(8,128)(2,1)} async-done(((bf16[32,64,128]{2,1,0:T(8,128)(2,1)}), bf16[32,256,128]{2,1,0:T(8,128)(2,1)}) %all-gather.8.cloned.1.call-update) | async-done | bytes 2097168 | tf_op jit(solution)/shard_map/all_gather | solution.py:30
  262.9 81.6 %all-gather.6.cloned.1.call-done = bf16[32,256,256]{2,1,0:T(8,128)(2,1)} async-done(((bf16[32,64,256]{2,1,0:T(8,128)(2,1)}), bf16[32,256,256]{2,1,0:T(8,128)(2,1)}) %all-gather.6.cloned.1.call-update) | async-done | bytes 4194320 | tf_op jit(solution)/shard_map/all_gather | solution.py:29
  344.4 4.2 %convolution_convert_fusion.1 = bf16[32,256,128]{2,1,0:T(8,128)(2,1)S(1)} fusion(bf16[32,256,256]{2,1,0:T(8,128)(2,1)} %all-gather.6.cloned.1.call-done, bf16[32,256,128]{2,1,0:T(8,128)(2,1)} %all-gather.8.cloned.1.call-done), kind=kOutput, calls=%fused_computation.5 | convolution fusion | flops 537919488 | bytes 8388608 | tf_op jit(solution)/shard_map/wik,wka->wia/dot_general | solution.py:33
  348.7 0.0 copy-done
  348.7 1.2 multiply_convert_fusion.1
  349.9 1.2 multiply_convert_fusion
  351.2 0.0 copy-start.1
  351.2 1.2 fusion.11
  352.5 1.4 convert_add_fusion
  (2 shorter events, 0.0 us)
Async XLA Ops:
  7.2 60.3 %all-gather.4.cloned.1.call-start = ((), (), s32[]{:S(2)}) async-start(), calls=%async_computation.1 | async-start | bytes 9437184 | tf_op jit(solution)/shard_map/all_gather | solution.py:14
  10.0 120.5 %all-reduce.2.cloned.1.call-start = ((), (), s32[]{:S(2)}) async-start(), calls=%async_computation.2 | async-start | bytes 524288 | tf_op jit(solution)/shard_map/psum | solution.py:19
  94.7 121.0 %reduce-scatter.2.cloned.1.call-start = ((), (), s32[]{:S(2)}) async-start(), calls=%async_computation.3 | async-start | bytes 9437184 | tf_op jit(solution)/shard_map/reduce_scatter | solution.py:21
  94.8 36.7 %copy-start.3 = (f32[256,512]{1,0:T(8,128)S(1)}, f32[256,512]{1,0:T(8,128)}, u32[]{:S(2)}) copy-start(f32[256,512]{1,0:T(8,128)} %param.6) | copy-start | bytes 1572868
  131.5 12.7 %copy-start.2 = (f32[256,512]{1,0:T(8,128)}, f32[256,512]{1,0:T(8,128)S(1)}, u32[]{:S(2)}) copy-start(f32[256,512]{1,0:T(8,128)S(1)} %convert_element_type.41) | copy-start | bytes 1572868
  144.2 118.7 %all-gather.8.cloned.1.call-start = ((), (), s32[]{:S(2)}) async-start(), calls=%async_computation.5 | async-start | bytes 2621440 | tf_op jit(solution)/shard_map/all_gather | solution.py:30
  144.8 199.6 %all-gather.6.cloned.1.call-start = ((), (), s32[]{:S(2)}) async-start(), calls=%async_computation.4 | async-start | bytes 5242880 | tf_op jit(solution)/shard_map/all_gather | solution.py:29
  344.4 4.3 %copy-start = (bf16[32,256,256]{2,1,0:T(8,128)(2,1)S(1)}, bf16[32,256,256]{2,1,0:T(8,128)(2,1)}, u32[]{:S(2)}) copy-start(bf16[32,256,256]{2,1,0:T(8,128)(2,1)} %all-gather.6.cloned.1.call-done) | copy-start | bytes 12582916
  351.2 1.3 copy-start.1
Sparse Core Ops, SparseCore 0:
  10.4 56.9 all-gather.3
  94.9 35.5 all-reduce.1
  144.3 71.3 reduce-scatter.1
  217.2 45.6 all-gather.7
  264.9 79.5 all-gather.5
where the time goes:
time: 361 us; the launch traced here: 360 us
  waiting for transfers between devices  273 us (76%)
  matrix products  47.9 us (13%)
  local copies, waits for them, and re-layouts  23.1 us (6%)
  between operations  13.9 us (4%)
    all_gather x1, waiting for transfers between devices, shards(): full_potential = lax.all_gather(potential, 'rows', axis=1, tiled=True)  81.6 us
    reduce_scatter x1, waiting for transfers between devices, shards(): lax.psum_scatter(jnp.dot(shifted, flat_chol, preferred_element_type=jnp.f...  70.7 us
    all_gather x1, waiting for transfers between devices, shards(): batch_piece = lax.all_gather(green, 'blk', axis=0, tiled=True)  57.4 us
    all_gather x1, waiting for transfers between devices, shards(): full_term = lax.all_gather(walker_orbitals, 'rows', axis=1, tiled=True)  44.7 us
    dot_general x1, matrix products, shards(): lax.dot_general(flat_piece, flat_chol, (((1,), (1,)), ((), ())), preferre...  27.3 us
    unnamed x11, local copies, waits for them, and re-layouts  23.1 us
    psum x1, waiting for transfers between devices, shards(): lax.psum(partial_bias.astype(jnp.bfloat16), 'rows').astype(jnp.float32)  17.8 us
    dot_general x1, matrix products, shards(): jnp.dot(shifted, flat_chol, preferred_element_type=jnp.float32)  12.7 us
  transfers between devices with their start and end apart: 5, of which 5 were waited for; matrix products, arithmetic and copies ran while one was open for 6% of the time, Pallas kernels for 0%

commit v1 on v0

--- a/solution.py
+++ b/solution.py
@@ -26,7 +26,14 @@
     )
     potential = summed.reshape(walk_count, rows_dev, orbitals)
     result = walker_orbitals.astype(jnp.float32)
-    full_potential = lax.all_gather(potential, "rows", axis=1, tiled=True)
+    devices = lax.axis_size("rows")
+    hops = [(i, (i + 1) % devices) for i in range(devices)]
+    blocks = [potential]
+    for far in range(1, devices):
+        blocks = [lax.ppermute(blocks[0], "rows", hops), *blocks]
+    whole = jnp.concatenate(blocks, axis=1)
+    shift = (lax.axis_index("rows") + 1) * blocks[-1].shape[1]
+    full_potential = jnp.roll(whole, shift, axis=1)
     full_term = lax.all_gather(walker_orbitals, "rows", axis=1, tiled=True)
     offset = lax.axis_index("rows") * rows_dev
     for degree in range(1, TAYLOR + 1):

time: 361 us -> 361 us (level)
  waiting for transfers between devices: 273 us -> 245 us
  local copies, waits for them, and re-layouts: 23.1 us -> 34.1 us
  starting transfers between devices: 0.42 us -> 10.3 us
  matrix products: 47.9 us -> 54.3 us
    ppermute x0 -> x3, waiting for transfers between devices: none -> 98.5 us  [shards(): blocks = [lax.ppermute(blocks[0], 'rows', hops), *blocks]]
    all_gather x1 -> x0, waiting for transfers between devices: 81.6 us -> none  [shards(): full_potential = lax.all_gather(potential, 'rows', axis=1, tiled=True)]
    all_gather x1, waiting for transfers between devices: 44.7 us -> 0.01 us  [shards(): full_term = lax.all_gather(walker_orbitals, 'rows', axis=1, tiled=True)]
    ppermute x0 -> x3, starting transfers between devices: none -> 10.1 us  [shards(): blocks = [lax.ppermute(blocks[0], 'rows', hops), *blocks]]
    unnamed x11 -> x16, local copies, waits for them, and re-layouts: 23.1 us -> 33.1 us
    dot_general x4, matrix products: 7.96 us -> 14.6 us  [shards(): jnp.einsum('wik,wka->wia', full_potential, full_term, preferred_element_t...]
  transfers between devices with their start and end apart: 5 -> 7, of which waited for: 5 -> 6; matrix products, arithmetic and copies ran while one was open for 6% -> 8% of each run, Pallas kernels for 0% -> 0%
where the time goes in v1:
time: 361 us; the launch traced here: 360 us
  waiting for transfers between devices  245 us (68%)
  matrix products  54.3 us (15%)
  local copies, waits for them, and re-layouts  34.1 us (9%)
  between operations  13.9 us (4%)
  starting transfers between devices  10.3 us (3%)
    ppermute x3, waiting for transfers between devices, shards(): blocks = [lax.ppermute(blocks[0], 'rows', hops), *blocks]  98.5 us
    reduce_scatter x1, waiting for transfers between devices, shards(): lax.psum_scatter(jnp.dot(shifted, flat_chol, preferred_element_type=jnp.f...  71.5 us
    all_gather x1, waiting for transfers between devices, shards(): batch_piece = lax.all_gather(green, 'blk', axis=0, tiled=True)  57.4 us
    unnamed x16, local copies, waits for them, and re-layouts  33.1 us
    dot_general x1, matrix products, shards(): lax.dot_general(flat_piece, flat_chol, (((1,), (1,)), ((), ())), preferre...  27.3 us
    psum x1, waiting for transfers between devices, shards(): lax.psum(partial_bias.astype(jnp.bfloat16), 'rows').astype(jnp.float32)  17.8 us
    dot_general x4, matrix products, shards(): jnp.einsum('wik,wka->wia', full_potential, full_term, preferred_element_t...  14.6 us
    dot_general x1, matrix products, shards(): jnp.dot(shifted, flat_chol, preferred_element_type=jnp.float32)  12.5 us
  transfers between devices with their start and end apart: 7, of which 6 were waited for; matrix products, arithmetic and copies ran while one was open for 8% of the time, Pallas kernels for 0%

profile of v1, /device:TPU:0, one launch (start us, length us, event | category | flops | bytes accessed | tf_op | source)
XLA Modules:
  0.0 360.2 jit_solution(14055277755142115653)
XLA Ops:
  7.2 0.0 all-gather.3.cloned.1.call-start
  7.2 2.8 copy.6
  10.0 0.0 all-reduce.2.cloned.1.call-start
  10.1 57.4 %all-gather.3.cloned.1.call-done = bf16[256,64,256]{2,0,1:T(8,128)(2,1)} async-done(((bf16[32,64,256]{2,0,1:T(8,128)(2,1)}), bf16[256,64,256]{2,0,1:T(8,128)(2,1)}) %all-gather.3.cloned.1.call-update) | async-done | bytes 8388624 | tf_op jit(solution)/shard_map/all_gather | solution.py:14
  67.5 27.3 %fusion.20 = bf16[256,512]{1,0:T(8,128)(2,1)} fusion(bf16[256,64,256]{2,0,1:T(8,128)(2,1)} %all-gather.3.cloned.1.call-done, bf16[512,64,256]{2,1,0:T(8,128)(2,1)} %param.4), kind=kOutput, calls=%fused_computation.15 | convolution fusion | flops 4295098368 | bytes 25427968 | tf_op jit(solution)/shard_map/dot_general | solution.py:16
  94.7 0.0 reduce-scatter.2.cloned.1.call-start
  94.8 17.9 %copy.8 = bf16[64,8,64,256]{3,1,2,0:T(8,128)(2,1)} copy(bf16[64,8,64,256]{3,2,1,0:T(8,128)(2,1)} %bitcast.15) | data formatting | bytes 33554432
  112.7 17.8 %all-reduce.2.cloned.1.call-done = bf16[256,512]{1,0:T(8,128)(2,1)} async-done(((bf16[256,512]{1,0:T(8,128)(2,1)}), bf16[256,512]{1,0:T(8,128)(2,1)}) %all-reduce.2.cloned.1.call-update) | async-done | bytes 262160 | tf_op jit(solution)/shard_map/psum | solution.py:19
  130.5 1.0 convert_element_type.41
  131.5 0.8 copy-done.1
  132.3 12.5 %convolution_convert_fusion = bf16[256,16384]{1,0:T(8,128)(2,1)} fusion(bf16[512,16384]{1,0:T(8,128)(2,1)} %bitcast.14, f32[256,512]{1,0:T(8,128)S(1)} %copy-done.2, f32[256,512]{1,0:T(8,128)S(1)} %convert_element_type.41), kind=kOutput, calls=%fused_computation | convolution fusion | flops 4299554816 | bytes 26214400 | tf_op jit(solution)/shard_map/dot_general | solution.py:22
  144.8 0.0 all-gather.5.cloned.1.call-start
  144.8 71.5 %reduce-scatter.2.cloned.1.call-done = bf16[32,16384]{1,0:T(8,128)(2,1)} async-done(((bf16[256,16384]{1,0:T(8,128)(2,1)}), bf16[32,16384]{1,0:T(8,128)(2,1)}) %reduce-scatter.2.cloned.1.call-update) | async-done | bytes 1048592 | tf_op jit(solution)/shard_map/reduce_scatter | solution.py:21
  216.3 1.5 copy.9
  217.8 1.5 collective-permute-start
  219.3 25.0 %collective-permute-done = bf16[32,64,256]{2,1,0:T(8,128)(2,1)S(1)} collective-permute-done((bf16[32,64,256]{2,1,0:T(8,128)(2,1)S(1)}, bf16[32,64,256]{2,1,0:T(8,128)(2,1)S(1)}, u32[]{:S(2)}, u32[]{:S(2)}) %collective-permute-start) | collective-permute-done | bytes 1048608 | tf_op jit(solution)/shard_map/ppermute | solution.py:33
  244.4 40.6 %collective-permute-done.1 = bf16[32,64,256]{2,1,0:T(8,128)(2,1)S(1)} collective-permute-done((bf16[32,64,256]{2,1,0:T(8,128)(2,1)S(1)}, bf16[32,64,256]{2,1,0:T(8,128)(2,1)S(1)}, u32[]{:S(2)}, u32[]{:S(2)}) %collective-permute-start.1) | collective-permute-done | bytes 1048608 | tf_op jit(solution)/shard_map/ppermute | solution.py:33
  285.0 8.5 %collective-permute-start.2 = (bf16[32,64,256]{2,1,0:T(8,128)(2,1)S(1)}, bf16[32,64,256]{2,1,0:T(8,128)(2,1)}, u32[]{:S(2)}, u32[]{:S(2)}) collective-permute-start(bf16[32,64,256]{2,1,0:T(8,128)(2,1)S(1)} %collective-permute-done.1), channel_id=1, source_target_pairs={{0,1},{1,2},{2,3},{3,0},{4,5},{5,6},{6,7},{7,4},{8,9},{9,10},{10,1... | collective-permute-start | bytes 3145736 | tf_op jit(solution)/shard_map/ppermute | solution.py:33
  293.5 32.9 %collective-permute-done.2 = bf16[32,64,256]{2,1,0:T(8,128)(2,1)} collective-permute-done((bf16[32,64,256]{2,1,0:T(8,128)(2,1)S(1)}, bf16[32,64,256]{2,1,0:T(8,128)(2,1)}, u32[]{:S(2)}, u32[]{:S(2)}) %collective-permute-start.2) | collective-permute-done | bytes 1048608 | tf_op jit(solution)/shard_map/ppermute | solution.py:33
  326.4 2.3 constant_dynamic-update-slice_fusion.7
  328.8 1.1 constant_dynamic-update-slice_fusion.6
  329.9 1.1 constant_dynamic-update-slice_fusion.5
  331.0 1.1 constant_dynamic-update-slice_fusion.4
  332.1 2.3 constant_dynamic-update-slice_fusion.3
  334.4 1.1 constant_dynamic-update-slice_fusion.2
  335.5 1.1 constant_dynamic-update-slice_fusion.1
  336.6 1.1 constant_dynamic-update-slice_fusion
  337.6 4.1 %fusion.10 = bf16[32,256,128]{2,1,0:T(8,128)(2,1)S(1)} fusion(bf16[32,256,128]{2,1,0:T(8,128)(2,1)} %all-gather.5.cloned.1.call-done, bf16[32,512,256]{2,1,0:T(8,128)(2,1)} %constant_dynamic-update-slice_fusion, s32[]{:T(128)S(6)} %select_n.20), kind=kOutput, calls=%fused_computation.13 | convolution fusion | flops 537919488 | bytes 8388612 | tf_op jit(solution)/shard_map/wik,wka->wia/dot_general | solution.py:40
  341.8 3.5 multiply_convert_fusion.1
  345.2 3.5 multiply_convert_fusion
  348.8 3.5 fusion.2
  352.2 1.4 convert_add_fusion
  (11 shorter events, 0.1 us)
Async XLA Ops:
  7.2 60.3 %all-gather.3.cloned.1.call-start = ((), (), s32[]{:S(2)}) async-start(), calls=%async_computation.1 | async-start | bytes 9437184 | tf_op jit(solution)/shard_map/all_gather | solution.py:14
  10.0 120.5 %all-reduce.2.cloned.1.call-start = ((), (), s32[]{:S(2)}) async-start(), calls=%async_computation.2 | async-start | bytes 524288 | tf_op jit(solution)/shard_map/psum | solution.py:19
  94.7 121.6 %reduce-scatter.2.cloned.1.call-start = ((), (), s32[]{:S(2)}) async-start(), calls=%async_computation.3 | async-start | bytes 9437184 | tf_op jit(solution)/shard_map/reduce_scatter | solution.py:21
  94.8 37.5 %copy-start.2 = (f32[256,512]{1,0:T(8,128)S(1)}, f32[256,512]{1,0:T(8,128)}, u32[]{:S(2)}) copy-start(f32[256,512]{1,0:T(8,128)} %param.6) | copy-start | bytes 1572868
  131.5 0.8 copy-start.1
  144.8 192.8 %all-gather.5.cloned.1.call-start = ((), (), s32[]{:S(2)}) async-start(), calls=%async_computation.4 | async-start | bytes 2621440 | tf_op jit(solution)/shard_map/all_gather | solution.py:37
  217.8 26.6 %collective-permute-start = (bf16[32,64,256]{2,1,0:T(8,128)(2,1)S(1)}, bf16[32,64,256]{2,1,0:T(8,128)(2,1)S(1)}, u32[]{:S(2)}, u32[]{:S(2)}) collective-permute-start(bf16[32,64,256]{2,1,0:T(8,128)(2,1)S(1)} %bitcast.16), channel_id=1, source_target_pairs={{0,1},{1,2},{2,3},{3,0},{4,5},{5,6},{6,7},{7,4},{8,9},{9,10},{10,1... | collective-permute-start | bytes 3145736 | tf_op jit(solution)/shard_map/ppermute | solution.py:33
  244.4 40.6 %collective-permute-start.1 = (bf16[32,64,256]{2,1,0:T(8,128)(2,1)S(1)}, bf16[32,64,256]{2,1,0:T(8,128)(2,1)S(1)}, u32[]{:S(2)}, u32[]{:S(2)}) collective-permute-start(bf16[32,64,256]{2,1,0:T(8,128)(2,1)S(1)} %collective-permute-done), channel_id=1, source_target_pairs={{0,1},{1,2},{2,3},{3,0},{4,5},{5,6},{6,7},{7,4},{8,9},{9,10},{10,1... | collective-permute-start | bytes 3145736 | tf_op jit(solution)/shard_map/ppermute | solution.py:33
  285.0 41.5 %collective-permute-start.2 = (bf16[32,64,256]{2,1,0:T(8,128)(2,1)S(1)}, bf16[32,64,256]{2,1,0:T(8,128)(2,1)}, u32[]{:S(2)}, u32[]{:S(2)}) collective-permute-start(bf16[32,64,256]{2,1,0:T(8,128)(2,1)S(1)} %collective-permute-done.1), channel_id=1, source_target_pairs={{0,1},{1,2},{2,3},{3,0},{4,5},{5,6},{6,7},{7,4},{8,9},{9,10},{10,1... | collective-permute-start | bytes 3145736 | tf_op jit(solution)/shard_map/ppermute | solution.py:33
  345.2 7.0 %copy-start = (bf16[32,64,128]{2,1,0:T(8,128)(2,1)S(1)}, bf16[32,64,128]{2,1,0:T(8,128)(2,1)}, u32[]{:S(2)}) copy-start(bf16[32,64,128]{2,1,0:T(8,128)(2,1)} %param.7) | copy-start | bytes 1572868
Sparse Core Ops, SparseCore 0:
  10.4 56.9 all-gather.2
  94.9 35.5 all-reduce.1
  144.9 71.3 reduce-scatter.1
  244.5 69.2 all-gather.4
